TPU v7x, 32 devices: a whole 2x2x4 slice. The times are simulated.
32 devices in a mesh: sp: 2 (over x), ep: 16 (over z, y, core).
Axes of the slice: x: 2, y: 2, z: 4, core: 2. Of those that a mesh axis runs over, the one named last changes fastest.
Arguments:
- activations: bfloat16 [16, 8, 3584], P('ep', 'sp'), may hold values from -6 to 6
- out_grad: bfloat16 [16, 8, 3584], P('ep', 'sp'), may hold values from -6 to 6
- route_weights: bfloat16 [16, 8, 8], P('ep', 'sp'), may hold values from 0.019897461 to 0.5
- expert_ids: int32 [16, 8, 8], P('ep', 'sp'), may hold values from 0 to 15, all different within a row; in each aligned block of 8 rows (0 to 7, 8 to 15, ..., all dimensions but the last counted through in order) at most 6 rows name the same one
- w_gate: bfloat16 [16, 3584, 1024], P('ep', None, 'sp'), may hold values from -0.09375 to 0.09375
- w_up: bfloat16 [16, 3584, 1024], P('ep', None, 'sp'), may hold values from -0.09375 to 0.09375
- w_down: bfloat16 [16, 1024, 3584], P('ep', 'sp'), may hold values from -0.1875 to 0.1875
Outputs:
- input_grad: bfloat16 [16, 8, 3584], P('ep', 'sp')
- w_down_grad: float32 [16, 1024, 3584], P('ep', 'sp')
Inputs may be any that keep to these rules, and one draw needn't show every extreme that they name: `expert_ids`: each row names 8 different experts. In each aligned block of 8 rows (one token group, the first two dimensions taken together) no expert is named by more than 6 rows, a bound that some block reaches.
All inputs are finite; a program needn't handle non-finite values.
Results may differ from a plain program's by a relative error of at most 0.014.
Values may be sent and summed in bfloat16 or wider, within the bound.
No kernel may reach another device: no remote copies, remote signals or barrier semaphores. Data moves between devices by JAX's collectives and lax.ppermute only.
A program may use at most 64 MiB of HBM per device.

v0:
```python
import jax
import jax.numpy as jnp
from jax import lax
from jax.sharding import PartitionSpec as P

TOP = 8


def expert_rows(rows_in, rows_grad, gate_w, up_w, down_w):
    gate_pre = jnp.dot(rows_in, gate_w, preferred_element_type=jnp.float32)
    up_pre = jnp.dot(rows_in, up_w, preferred_element_type=jnp.float32)
    squash = jax.nn.sigmoid(gate_pre)
    swish = gate_pre * squash
    hidden = (swish * up_pre).astype(jnp.bfloat16)
    hidden_grad = lax.dot_general(
        rows_grad, down_w, (((1,), (1,)), ((), ())), preferred_element_type=jnp.float32
    )
    gate_grad = (hidden_grad * up_pre * squash * (1.0 + gate_pre * (1.0 - squash))).astype(
        jnp.bfloat16
    )
    up_grad = (hidden_grad * swish).astype(jnp.bfloat16)
    first = lax.dot_general(
        gate_grad, gate_w, (((1,), (1,)), ((), ())), preferred_element_type=jnp.float32
    )
    second = lax.dot_general(
        up_grad, up_w, (((1,), (1,)), ((), ())), preferred_element_type=jnp.float32
    )
    partial_rows = (first + second).astype(jnp.bfloat16)
    weight_grad = lax.dot_general(
        hidden, rows_grad, (((0,), (0,)), ((), ())), preferred_element_type=jnp.float32
    )
    return (partial_rows, weight_grad)


def per_device(activations, out_grad, route_weights, expert_ids, w_gate, w_up, w_down):
    n_expert = lax.axis_size("ep")
    n_group = lax.axis_size("sp")
    tok_dev = activations.shape[1]
    width = activations.shape[2]
    capacity = max(2, tok_dev * n_group * TOP * 3 // (2 * n_expert))
    group_ids = lax.all_gather(expert_ids, "sp", axis=1, tiled=True)
    group_in, group_grad, group_weight = (
        lax.all_gather(activations, "sp", axis=1, tiled=True),
        lax.all_gather(out_grad, "sp", axis=1, tiled=True),
        lax.all_gather(route_weights, "sp", axis=1, tiled=True),
    )
    send_width = group_in.shape[2]
    tok_grp = group_ids.shape[1]
    slot_expert = group_ids[0].reshape(-1)
    slot_token = jnp.arange(slot_expert.shape[0], dtype=jnp.int32) // TOP
    onehot = (slot_expert[:, None] == jnp.arange(n_expert, dtype=jnp.int32)[None, :]).astype(
        jnp.int32
    )
    before = jnp.cumsum(onehot, axis=0) - onehot
    rank = jnp.sum(before * onehot, axis=1)
    position = slot_expert * capacity + rank
    total_rows = n_expert * capacity
    token_in = group_in[0][slot_token]
    scaled = (
        group_weight[0].reshape(-1).astype(jnp.float32)[:, None]
        * group_grad[0][slot_token].astype(jnp.float32)
    ).astype(jnp.bfloat16)
    send_in = (
        jnp.zeros((total_rows, send_width), jnp.bfloat16)
        .at[position]
        .set(token_in)
        .reshape(n_expert, capacity, send_width)
    )
    send_grad = (
        jnp.zeros((total_rows, send_width), jnp.bfloat16)
        .at[position]
        .set(scaled)
        .reshape(n_expert, capacity, send_width)
    )
    recv_in, recv_grad = (
        lax.all_to_all(send_in, "ep", split_axis=0, concat_axis=0, tiled=True),
        lax.all_to_all(send_grad, "ep", split_axis=0, concat_axis=0, tiled=True),
    )
    flat_in = recv_in.reshape(total_rows, width)
    flat_grad = recv_grad.reshape(total_rows, width)
    gate_w = w_gate[0]
    up_w = w_up[0]
    down_w = w_down[0]
    partial_rows, weight_grad = expert_rows(flat_in, flat_grad, gate_w, up_w, down_w)
    partial_rows = partial_rows.reshape(n_expert, capacity, width)
    slot_owner = jnp.full((total_rows,), -1, jnp.int32).at[position].set(slot_token)
    owner_match = jnp.arange(tok_grp, dtype=jnp.int32)[:, None] == slot_owner[None, :]
    back_rows = lax.all_to_all(partial_rows, "ep", split_axis=0, concat_axis=0, tiled=True)
    token_sum = jnp.dot(
        owner_match.astype(jnp.bfloat16),
        back_rows.reshape(total_rows, width),
        preferred_element_type=jnp.float32,
    )
    own_sum = lax.psum_scatter(
        token_sum.astype(jnp.bfloat16), "sp", scatter_dimension=0, tiled=True
    )
    return (own_sum.reshape(1, tok_dev, width), weight_grad[None])


def solution(mesh):
    return jax.shard_map(
        per_device,
        mesh=mesh,
        in_specs=(
            P("ep", "sp", None),
            P("ep", "sp", None),
            P("ep", "sp", None),
            P("ep", "sp", None),
            P("ep", None, "sp"),
            P("ep", None, "sp"),
            P("ep", "sp", None),
        ),
        out_specs=(P("ep", "sp", None), P("ep", "sp", None)),
        check_vma=False,
    )
```

profile of v0, /device:TPU:16, one launch (start us, length us, event | category | flops | bytes accessed | tf_op | source)
XLA Modules:
  0.0 116.9 jit_solution(2344344698198534478)
XLA Ops:
  0.7 4.5 %all_gather.12 = s32[1,8,8]{2,0,1:T(1,128)S(1)} all-gather(s32[1,4,8]{2,0,1:T(1,128)} %bitcast.44), channel_id=1, replica_groups=mesh['sp'=2,'ep'=16] {'sp'}, dimensions={1}, use_global_device_ids=true | all-gather | bytes 384 | tf_op jit(solution)/shard_map/all_gather | solution.py:41
  6.9 0.8 copy.16
  7.7 4.8 %all_gather.15 = bf16[1,8,3584]{2,0,1:T(2,128)(2,1)S(1)} all-gather(bf16[1,4,3584]{2,0,1:T(2,128)(2,1)S(1)} %copy.16), channel_id=1, replica_groups=mesh['sp'=2,'ep'=16] {'sp'}, dimensions={1}, use_global_device_ids=true | all-gather | bytes 86016 | tf_op jit(solution)/shard_map/all_gather | solution.py:43
  12.6 2.8 %scatter_custom_fusion.2 = bf16[96,3584]{1,0:T(8,128)(2,1)S(1)} fusion(s32[64]{0:T(128)S(1)} %fusion.23, bf16[8,3584]{1,0:T(8,128)(2,1)S(1)} %bitcast.43, s32[1024]{0:T(1024)S(1)} %pad_clamp_fusion, bf16[]{:T(256)} %constant.34.clone.1), kind=kCustom, calls=%fused_computation.20 | custom fusion | bytes 688130 | tf_op jit(solution)/shard_map/scatter | solution.py:66
  15.4 1.2 reshape.107
  16.5 6.2 %all-to-all-start.1 = ((bf16[16,6,3584]{2,1,0:T(8,128)(2,1)}), bf16[16,6,3584]{2,1,0:T(8,128)(2,1)S(1)}, u32[]{:S(2)}, u32[]{:S(2)}) async-start(bf16[16,6,3584]{2,1,0:T(8,128)(2,1)} %reshape.107), calls=%async_computation.1 | async-start | bytes 1835008 | tf_op jit(solution)/shard_map/all_to_all | solution.py:76
  22.7 4.4 %all_gather.13 = bf16[1,8,8]{2,0,1:T(2,128)(2,1)S(1)} all-gather(bf16[1,4,8]{2,0,1:T(2,128)(2,1)S(1)} %copy.14), channel_id=1, replica_groups=mesh['sp'=2,'ep'=16] {'sp'}, dimensions={1}, use_global_device_ids=true | all-gather | bytes 192 | tf_op jit(solution)/shard_map/all_gather | solution.py:45
  27.2 4.8 %all_gather.14 = bf16[1,8,3584]{2,0,1:T(2,128)(2,1)S(1)} all-gather(bf16[1,4,3584]{2,0,1:T(2,128)(2,1)S(1)} %copy.15), channel_id=1, replica_groups=mesh['sp'=2,'ep'=16] {'sp'}, dimensions={1}, use_global_device_ids=true | all-gather | bytes 86016 | tf_op jit(solution)/shard_map/all_gather | solution.py:44
  32.1 2.9 %scatter_custom_fusion.1 = bf16[96,3584]{1,0:T(8,128)(2,1)S(1)} fusion(s32[64]{0:T(128)S(1)} %fusion.23, f32[64]{0:T(128)S(1)} %reshape.112, bf16[]{:T(256)} %constant.34.clone.1, bf16[8,3584]{1,0:T(8,128)(2,1)S(1)} %bitcast.42, s32[1024]{0:T(1024)S(1)} %pad_clamp_fusion), kind=kCustom, calls=%fused_computation.19 | custom fusion | flops 688128 | bytes 750082 | tf_op jit(solution)/shard_map/scatter | solution.py:72
  35.0 1.2 reshape.105
  36.1 8.9 %all-to-all-done.1 = bf16[16,6,3584]{2,1,0:T(8,128)(2,1)S(1)} async-done(((bf16[16,6,3584]{2,1,0:T(8,128)(2,1)}), bf16[16,6,3584]{2,1,0:T(8,128)(2,1)S(1)}, u32[]{:S(2)}, u32[]{:S(2)}) %all-to-all-start.1) | async-done | bytes 688160 | tf_op jit(solution)/shard_map/all_to_all | solution.py:76
  45.0 4.5 %all-to-all-start = ((bf16[16,6,3584]{2,1,0:T(8,128)(2,1)}), bf16[16,6,3584]{2,1,0:T(8,128)(2,1)S(1)}, u32[]{:S(2)}, u32[]{:S(2)}) async-start(bf16[16,6,3584]{2,1,0:T(8,128)(2,1)} %reshape.105), calls=%async_computation | async-start | bytes 1835008 | tf_op jit(solution)/shard_map/all_to_all | solution.py:77
  49.8 2.9 %fusion.3 = f32[96,512]{1,0:T(8,128)S(1)} fusion(bf16[96,3584]{1,0:T(8,128)(2,1)S(1)} %reshape.108, bf16[1,3584,512]{2,1,0:T(8,128)(2,1)} %param.11), kind=kOutput, calls=%fused_computation.11 | convolution fusion | flops 352321536 | bytes 4554752 | tf_op jit(solution)/shard_map/dot_general | solution.py:10
  53.7 18.2 %all-to-all-done = bf16[16,6,3584]{2,1,0:T(8,128)(2,1)S(1)} async-done(((bf16[16,6,3584]{2,1,0:T(8,128)(2,1)}), bf16[16,6,3584]{2,1,0:T(8,128)(2,1)S(1)}, u32[]{:S(2)}, u32[]{:S(2)}) %all-to-all-start) | async-done | bytes 688160 | tf_op jit(solution)/shard_map/all_to_all | solution.py:77
  72.2 3.4 %fusion.8 = f32[96,512]{1,0:T(8,128)S(1)} fusion(bf16[96,3584]{1,0:T(8,128)(2,1)S(1)} %reshape.106, bf16[1,512,3584]{2,1,0:T(8,128)(2,1)} %param.13), kind=kOutput, calls=%fused_computation.16 | convolution fusion | flops 352321536 | bytes 4554752 | tf_op jit(solution)/shard_map/dot_general | solution.py:15
  75.6 1.2 %fusion.1 = f32[96,3584]{1,0:T(8,128)S(1)} fusion(bf16[1,3584,512]{2,1,0:T(8,128)(2,1)S(1)} %copy-done, f32[96,512]{1,0:T(8,128)S(1)} %fusion.3, f32[96,512]{1,0:T(8,128)S(1)} %fusion.8, f32[96,512]{1,0:T(8,128)S(1)} %fusion.6), kind=kOutput, calls=%fused_computation.9 | convolution fusion | flops 352813056 | bytes 5636096 | tf_op jit(solution)/shard_map/dot_general | solution.py:22
  76.8 0.8 copy-done.2
  77.6 1.2 %fusion = bf16[96,3584]{1,0:T(8,128)(2,1)S(1)} fusion(f32[96,3584]{1,0:T(8,128)S(1)} %fusion.1, bf16[1,3584,512]{2,1,0:T(8,128)(2,1)S(1)} %copy-done.2, f32[96,512]{1,0:T(8,128)S(1)} %fusion.8, f32[96,512]{1,0:T(8,128)S(1)} %fusion.3), kind=kOutput, calls=%fused_computation.7 | convolution fusion | flops 353304576 | bytes 6127616 | tf_op jit(solution)/shard_map/dot_general | solution.py:25
  78.9 1.2 reshape.109
  80.0 4.5 %all-to-all-start.2 = ((bf16[16,6,3584]{2,1,0:T(8,128)(2,1)}), bf16[16,6,3584]{2,1,0:T(8,128)(2,1)S(1)}, u32[]{:S(2)}, u32[]{:S(2)}) async-start(bf16[16,6,3584]{2,1,0:T(8,128)(2,1)} %reshape.109), calls=%async_computation.2 | async-start | bytes 1835008 | tf_op jit(solution)/shard_map/all_to_all | solution.py:88
  85.8 0.8 scatter_custom_fusion
  86.6 4.2 %convolution_bitcast_fusion = f32[1,512,3584]{2,1,0:T(8,128)} fusion(bf16[96,3584]{1,0:T(8,128)(2,1)S(1)} %reshape.106, f32[96,512]{1,0:T(8,128)S(1)} %fusion.6, f32[96,512]{1,0:T(8,128)S(1)} %fusion.3), kind=kOutput, calls=%fused_computation.5 | convolution fusion | flops 352616448 | bytes 8421376 | tf_op jit(solution)/shard_map/dot_general | solution.py:29
  90.8 16.1 %all-to-all-done.2 = bf16[16,6,3584]{2,1,0:T(8,128)(2,1)S(1)} async-done(((bf16[16,6,3584]{2,1,0:T(8,128)(2,1)}), bf16[16,6,3584]{2,1,0:T(8,128)(2,1)S(1)}, u32[]{:S(2)}, u32[]{:S(2)}) %all-to-all-start.2) | async-done | bytes 688160 | tf_op jit(solution)/shard_map/all_to_all | solution.py:88
  107.3 9.0 %all-reduce = bf16[8,3584]{1,0:T(8,128)(2,1)S(1)} all-reduce(bf16[8,3584]{1,0:T(8,128)(2,1)S(1)} %convolution_convert_fusion), channel_id=2, replica_groups=mesh['sp'=2,'ep'=16] {'sp'}, use_global_device_ids=true, to_apply=%region_5.6.clone | all-reduce | flops 28672 | bytes 114688
  (35 shorter events, 4.9 us)
Async XLA Ops:
  0.6 22.1 %copy-start.4 = (bf16[1,4,8]{2,1,0:T(4,128)(2,1)S(1)}, bf16[1,4,8]{2,1,0:T(4,128)(2,1)}, u32[]{:S(2)}) copy-start(bf16[1,4,8]{2,1,0:T(4,128)(2,1)} %param.9) | copy-start | bytes 196
  0.6 26.6 %copy-start.3 = (bf16[1,4,3584]{2,1,0:T(4,128)(2,1)S(1)}, bf16[1,4,3584]{2,1,0:T(4,128)(2,1)}, u32[]{:S(2)}) copy-start(bf16[1,4,3584]{2,1,0:T(4,128)(2,1)} %param.8) | copy-start | bytes 86020
  16.5 28.5 %all-to-all-start.1 = ((bf16[16,6,3584]{2,1,0:T(8,128)(2,1)}), bf16[16,6,3584]{2,1,0:T(8,128)(2,1)S(1)}, u32[]{:S(2)}, u32[]{:S(2)}) async-start(bf16[16,6,3584]{2,1,0:T(8,128)(2,1)} %reshape.107), calls=%async_computation.1 | async-start | bytes 1835008 | tf_op jit(solution)/shard_map/all_to_all | solution.py:76
  45.0 26.9 %all-to-all-start = ((bf16[16,6,3584]{2,1,0:T(8,128)(2,1)}), bf16[16,6,3584]{2,1,0:T(8,128)(2,1)S(1)}, u32[]{:S(2)}, u32[]{:S(2)}) async-start(bf16[16,6,3584]{2,1,0:T(8,128)(2,1)} %reshape.105), calls=%async_computation | async-start | bytes 1835008 | tf_op jit(solution)/shard_map/all_to_all | solution.py:77
  49.8 3.1 %copy-start.1 = (bf16[1,3584,512]{2,1,0:T(8,128)(2,1)S(1)}, bf16[1,3584,512]{2,1,0:T(8,128)(2,1)}, u32[]{:S(2)}) copy-start(bf16[1,3584,512]{2,1,0:T(8,128)(2,1)} %param.12) | copy-start | bytes 11010052
  72.1 3.4 %copy-start = (bf16[1,3584,512]{2,1,0:T(8,128)(2,1)S(1)}, bf16[1,3584,512]{2,1,0:T(8,128)(2,1)}, u32[]{:S(2)}) copy-start(bf16[1,3584,512]{2,1,0:T(8,128)(2,1)} %param.11) | copy-start | bytes 11010052
  75.6 2.0 %copy-start.2 = (bf16[1,3584,512]{2,1,0:T(8,128)(2,1)S(1)}, bf16[1,3584,512]{2,1,0:T(8,128)(2,1)}, u32[]{:S(2)}) copy-start(bf16[1,3584,512]{2,1,0:T(8,128)(2,1)} %param.12) | copy-start | bytes 11010052
  77.6 7.0 %copy-start.5 = (u32[32]{0:T(128)S(1)}, u32[32]{0:T(128)}, u32[]{:S(2)}) copy-start(u32[32]{0:T(128)} %constant.46) | copy-start | bytes 388
  80.0 26.9 %all-to-all-start.2 = ((bf16[16,6,3584]{2,1,0:T(8,128)(2,1)}), bf16[16,6,3584]{2,1,0:T(8,128)(2,1)S(1)}, u32[]{:S(2)}, u32[]{:S(2)}) async-start(bf16[16,6,3584]{2,1,0:T(8,128)(2,1)} %reshape.109), calls=%async_computation.2 | async-start | bytes 1835008 | tf_op jit(solution)/shard_map/all_to_all | solution.py:88
where the time goes:
time: 118 us; the launch traced here: 117 us
  waiting for transfers between devices  43.3 us (37%)
  blocking collectives  27.5 us (23%)
  starting transfers between devices  15.3 us (13%)
  matrix products  13.9 us (12%)
  local copies, waits for them, and re-layouts  11.6 us (10%)
  other arithmetic  3.92 us (3%)
  between operations  1.49 us (1%)
    all_to_all x1, waiting for transfers between devices, per_device(): lax.all_to_all(send_grad, 'ep', split_axis=0, concat_axis=0, tiled=True)  18.2 us
    all_to_all x1, waiting for transfers between devices, per_device(): lax.all_to_all(partial_rows, 'ep', split_axis=0, concat_axis=0, tiled=True)  16.1 us
    unnamed x1, blocking collectives  8.96 us
    all_to_all x1, waiting for transfers between devices, per_device(): lax.all_to_all(send_in, 'ep', split_axis=0, concat_axis=0, tiled=True)  8.92 us
    all_to_all x1, starting transfers between devices, per_device(): lax.all_to_all(send_in, 'ep', split_axis=0, concat_axis=0, tiled=True)  6.18 us
    all_gather x1, blocking collectives, per_device(): lax.all_gather(activations, 'sp', axis=1, tiled=True)  4.85 us
    all_gather x1, blocking collectives, per_device(): lax.all_gather(out_grad, 'sp', axis=1, tiled=True)  4.85 us
    all_to_all x1, starting transfers between devices, per_device(): lax.all_to_all(send_grad, 'ep', split_axis=0, concat_axis=0, tiled=True)  4.53 us
  transfers between devices with their start and end apart: 3, of which 3 were waited for; matrix products, arithmetic and copies ran while one was open for 12% of the time, Pallas kernels for 0%

commit v1 on v0

--- a/solution.py
+++ b/solution.py
@@ -4,6 +4,22 @@
 from jax.sharding import PartitionSpec as P
 
 TOP = 8
+
+
+def pairwise_exchange(x, axis, split, join):
+    ways, here = (lax.axis_size(axis), lax.axis_index(axis))
+    width = x.shape[split] // ways
+    lengths = list(x.shape)
+    lengths[split] = width
+    height = lengths[join]
+    lengths[join] = height * ways
+    full = jnp.zeros(lengths, x.dtype)
+    for mask in range(ways):
+        part = lax.dynamic_slice_in_dim(x, (here ^ mask) * width, width, axis=split)
+        if mask:
+            part = lax.ppermute(part, axis, [(d, d ^ mask) for d in range(ways)])
+        full = lax.dynamic_update_slice_in_dim(full, part, (here ^ mask) * height, axis=join)
+    return full
 
 
 def expert_rows(rows_in, rows_grad, gate_w, up_w, down_w):
@@ -73,7 +89,7 @@
         .reshape(n_expert, capacity, send_width)
     )
     recv_in, recv_grad = (
-        lax.all_to_all(send_in, "ep", split_axis=0, concat_axis=0, tiled=True),
+        pairwise_exchange(send_in, "ep", 0, 0),
         lax.all_to_all(send_grad, "ep", split_axis=0, concat_axis=0, tiled=True),
     )
     flat_in = recv_in.reshape(total_rows, width)

time: 118 us -> 149 us (1.26)
  starting transfers between devices: 15.3 us -> 36.7 us
  waiting for transfers between devices: 43.3 us -> 53 us
    ppermute x0 -> x15, waiting for transfers between devices: none -> 36.9 us  [pairwise_exchange(): part = lax.ppermute(part, axis, [(d, d ^ mask) for d in range(ways)])]
    ppermute x0 -> x15, starting transfers between devices: none -> 24.1 us  [pairwise_exchange(): part = lax.ppermute(part, axis, [(d, d ^ mask) for d in range(ways)])]
    all_to_all x1, waiting for transfers between devices: 18.2 us -> 0.01 us  [per_device(): lax.all_to_all(send_grad, 'ep', split_axis=0, concat_axis=0, tiled=True)]
    all_to_all x1 -> x0, waiting for transfers between devices: 8.92 us -> none  [per_device(): lax.all_to_all(send_in, 'ep', split_axis=0, concat_axis=0, tiled=True)]
    all_to_all x1 -> x0, starting transfers between devices: 6.18 us -> none  [per_device(): lax.all_to_all(send_in, 'ep', split_axis=0, concat_axis=0, tiled=True)]
    all_to_all x1, starting transfers between devices: 4.53 us -> 6.44 us  [per_device(): lax.all_to_all(partial_rows, 'ep', split_axis=0, concat_axis=0, tiled=True)]
    all_to_all x1, starting transfers between devices: 4.53 us -> 6.18 us  [per_device(): lax.all_to_all(send_grad, 'ep', split_axis=0, concat_axis=0, tiled=True)]
    unnamed x18 -> x16, local copies, waits for them, and re-layouts: 2.5 us -> 3.17 us
  transfers between devices with their start and end apart: 3 -> 17, of which waited for: 3 -> 11; matrix products, arithmetic and copies ran while one was open for 12% -> 9% of each run, Pallas kernels for 0% -> 0%
where the time goes in v1:
time: 149 us; the launch traced here: 148 us
  waiting for transfers between devices  53 us (36%)
  starting transfers between devices  36.7 us (25%)
  blocking collectives  27.5 us (18%)
  matrix products  13.9 us (9%)
  local copies, waits for them, and re-layouts  11.7 us (8%)
  other arithmetic  3.91 us (3%)
  between operations  1.75 us (1%)
    ppermute x15, waiting for transfers between devices, pairwise_exchange(): part = lax.ppermute(part, axis, [(d, d ^ mask) for d in range(ways)])  36.9 us
    ppermute x15, starting transfers between devices, pairwise_exchange(): part = lax.ppermute(part, axis, [(d, d ^ mask) for d in range(ways)])  24.1 us
    all_to_all x1, waiting for transfers between devices, per_device(): lax.all_to_all(partial_rows, 'ep', split_axis=0, concat_axis=0, tiled=True)  16.1 us
    unnamed x1, blocking collectives  8.96 us
    all_to_all x1, starting transfers between devices, per_device(): lax.all_to_all(partial_rows, 'ep', split_axis=0, concat_axis=0, tiled=True)  6.44 us
    all_to_all x1, starting transfers between devices, per_device(): lax.all_to_all(send_grad, 'ep', split_axis=0, concat_axis=0, tiled=True)  6.18 us
    all_gather x1, blocking collectives, per_device(): lax.all_gather(activations, 'sp', axis=1, tiled=True)  4.85 us
    all_gather x1, blocking collectives, per_device(): lax.all_gather(out_grad, 'sp', axis=1, tiled=True)  4.85 us
  transfers between devices with their start and end apart: 17, of which 11 were waited for; matrix products, arithmetic and copies ran while one was open for 9% of the time, Pallas kernels for 0%

profile of v1, /device:TPU:16, one launch (start us, length us, event | category | flops | bytes accessed | tf_op | source)
XLA Modules:
  0.0 148.4 jit_solution(7617024376013938534)
XLA Ops:
  1.4 4.5 %all_gather.12 = s32[1,8,8]{2,0,1:T(1,128)S(1)} all-gather(s32[1,4,8]{2,0,1:T(1,128)} %bitcast.44), channel_id=1, replica_groups=mesh['sp'=2,'ep'=16] {'sp'}, dimensions={1}, use_global_device_ids=true | all-gather | bytes 384 | tf_op jit(solution)/shard_map/all_gather | solution.py:57
  8.4 4.8 %all_gather.15 = bf16[1,8,3584]{2,0,1:T(2,128)(2,1)S(1)} all-gather(bf16[1,4,3584]{2,0,1:T(2,128)(2,1)S(1)} %copy.16), channel_id=1, replica_groups=mesh['sp'=2,'ep'=16] {'sp'}, dimensions={1}, use_global_device_ids=true | all-gather | bytes 86016 | tf_op jit(solution)/shard_map/all_gather | solution.py:59
  13.3 2.8 %scatter_custom_fusion.2 = bf16[96,3584]{1,0:T(8,128)(2,1)S(1)} fusion(s32[64]{0:T(128)S(1)} %get-tuple-element.21, bf16[8,3584]{1,0:T(8,128)(2,1)S(1)} %bitcast.43, s32[1024]{0:T(1024)S(1)} %pad_clamp_fusion, bf16[]{:T(256)} %constant.16.clone.1), kind=kCustom, calls=%fused_computation.20 | custom fusion | bytes 688130 | tf_op jit(solution)/shard_map/scatter | solution.py:82
  16.7 4.4 %all_gather.13 = bf16[1,8,8]{2,0,1:T(2,128)(2,1)S(1)} all-gather(bf16[1,4,8]{2,0,1:T(2,128)(2,1)S(1)} %copy.14), channel_id=1, replica_groups=mesh['sp'=2,'ep'=16] {'sp'}, dimensions={1}, use_global_device_ids=true | all-gather | bytes 192 | tf_op jit(solution)/shard_map/all_gather | solution.py:61
  21.2 4.8 %all_gather.14 = bf16[1,8,3584]{2,0,1:T(2,128)(2,1)S(1)} all-gather(bf16[1,4,3584]{2,0,1:T(2,128)(2,1)S(1)} %copy.15), channel_id=1, replica_groups=mesh['sp'=2,'ep'=16] {'sp'}, dimensions={1}, use_global_device_ids=true | all-gather | bytes 86016 | tf_op jit(solution)/shard_map/all_gather | solution.py:60
  26.1 2.9 %scatter_custom_fusion.1 = bf16[96,3584]{1,0:T(8,128)(2,1)S(1)} fusion(s32[64]{0:T(128)S(1)} %get-tuple-element.21, f32[64]{0:T(128)S(1)} %reshape.112, bf16[]{:T(256)} %constant.16.clone.1, bf16[8,3584]{1,0:T(8,128)(2,1)S(1)} %bitcast.42, s32[1024]{0:T(1024)S(1)} %pad_clamp_fusion), kind=kCustom, calls=%fused_computation.19 | custom fusion | flops 688128 | bytes 750082 | tf_op jit(solution)/shard_map/scatter | solution.py:88
  30.1 6.2 %all-to-all-start = ((bf16[16,6,3584]{2,1,0:T(8,128)(2,1)}), bf16[16,6,3584]{2,1,0:T(8,128)(2,1)S(1)}, u32[]{:S(2)}, u32[]{:S(2)}) async-start(bf16[16,6,3584]{2,1,0:T(8,128)(2,1)} %reshape.105), calls=%async_computation | async-start | bytes 1835008 | tf_op jit(solution)/shard_map/all_to_all | solution.py:93
  42.1 3.5 %collective-permute-done.1 = bf16[1,6,3584]{2,1,0:T(8,128)(2,1)S(1)} collective-permute-done((bf16[1,6,3584]{2,1,0:T(8,128)(2,1)S(1)}, bf16[1,6,3584]{2,1,0:T(8,128)(2,1)S(1)}, u32[]{:S(2)}, u32[]{:S(2)}) %collective-permute-start.1) | collective-permute-done | bytes 43040 | tf_op jit(solution)/shard_map/ppermute | solution.py:20
  45.7 4.4 %collective-permute-done.2 = bf16[1,6,3584]{2,1,0:T(8,128)(2,1)S(1)} collective-permute-done((bf16[1,6,3584]{2,1,0:T(8,128)(2,1)S(1)}, bf16[1,6,3584]{2,1,0:T(8,128)(2,1)S(1)}, u32[]{:S(2)}, u32[]{:S(2)}) %collective-permute-start.2) | collective-permute-done | bytes 43040 | tf_op jit(solution)/shard_map/ppermute | solution.py:20
  50.1 6.6 %collective-permute-start.3 = (bf16[1,6,3584]{2,1,0:T(8,128)(2,1)S(1)}, bf16[1,6,3584]{2,1,0:T(8,128)(2,1)S(1)}, u32[]{:S(2)}, u32[]{:S(2)}) collective-permute-start(bf16[1,6,3584]{2,1,0:T(8,128)(2,1)S(1)} %get-tuple-element.15), channel_id=1, source_target_pairs={{0,4},{1,5},{2,6},{3,7},{4,0},{5,1},{6,2},{7,3},{8,12},{9,13},{10,... | collective-permute-start | bytes 129032 | tf_op jit(solution)/shard_map/ppermute | solution.py:20
  56.7 3.3 %collective-permute-done.3 = bf16[1,6,3584]{2,1,0:T(8,128)(2,1)S(1)} collective-permute-done((bf16[1,6,3584]{2,1,0:T(8,128)(2,1)S(1)}, bf16[1,6,3584]{2,1,0:T(8,128)(2,1)S(1)}, u32[]{:S(2)}, u32[]{:S(2)}) %collective-permute-start.3) | collective-permute-done | bytes 43040 | tf_op jit(solution)/shard_map/ppermute | solution.py:20
  60.0 3.9 %collective-permute-done.4 = bf16[1,6,3584]{2,1,0:T(8,128)(2,1)S(1)} collective-permute-done((bf16[1,6,3584]{2,1,0:T(8,128)(2,1)S(1)}, bf16[1,6,3584]{2,1,0:T(8,128)(2,1)S(1)}, u32[]{:S(2)}, u32[]{:S(2)}) %collective-permute-start.4) | collective-permute-done | bytes 43040 | tf_op jit(solution)/shard_map/ppermute | solution.py:20
  64.0 4.9 %collective-permute-start.5 = (bf16[1,6,3584]{2,1,0:T(8,128)(2,1)S(1)}, bf16[1,6,3584]{2,1,0:T(8,128)(2,1)S(1)}, u32[]{:S(2)}, u32[]{:S(2)}) collective-permute-start(bf16[1,6,3584]{2,1,0:T(8,128)(2,1)S(1)} %get-tuple-element.13), channel_id=1, source_target_pairs={{0,6},{1,7},{2,4},{3,5},{4,2},{5,3},{6,0},{7,1},{8,14},{9,15},{10,... | collective-permute-start | bytes 129032 | tf_op jit(solution)/shard_map/ppermute | solution.py:20
  72.4 3.1 %collective-permute-done.6 = bf16[1,6,3584]{2,1,0:T(8,128)(2,1)S(1)} collective-permute-done((bf16[1,6,3584]{2,1,0:T(8,128)(2,1)S(1)}, bf16[1,6,3584]{2,1,0:T(8,128)(2,1)S(1)}, u32[]{:S(2)}, u32[]{:S(2)}) %collective-permute-start.6) | collective-permute-done | bytes 43040 | tf_op jit(solution)/shard_map/ppermute | solution.py:20
  77.4 3.3 %collective-permute-done.7 = bf16[1,6,3584]{2,1,0:T(8,128)(2,1)S(1)} collective-permute-done((bf16[1,6,3584]{2,1,0:T(8,128)(2,1)S(1)}, bf16[1,6,3584]{2,1,0:T(8,128)(2,1)S(1)}, u32[]{:S(2)}, u32[]{:S(2)}) %collective-permute-start.7) | collective-permute-done | bytes 43040 | tf_op jit(solution)/shard_map/ppermute | solution.py:20
  80.7 4.8 %collective-permute-done.8 = bf16[1,6,3584]{2,1,0:T(8,128)(2,1)S(1)} collective-permute-done((bf16[1,6,3584]{2,1,0:T(8,128)(2,1)S(1)}, bf16[1,6,3584]{2,1,0:T(8,128)(2,1)S(1)}, u32[]{:S(2)}, u32[]{:S(2)}) %collective-permute-start.8) | collective-permute-done | bytes 43040 | tf_op jit(solution)/shard_map/ppermute | solution.py:20
  85.5 3.5 %collective-permute-start.9 = (bf16[1,6,3584]{2,1,0:T(8,128)(2,1)S(1)}, bf16[1,6,3584]{2,1,0:T(8,128)(2,1)S(1)}, u32[]{:S(2)}, u32[]{:S(2)}) collective-permute-start(bf16[1,6,3584]{2,1,0:T(8,128)(2,1)S(1)} %get-tuple-element.9), channel_id=1, source_target_pairs={{0,10},{1,11},{2,8},{3,9},{4,14},{5,15},{6,12},{7,13},{8,2},{9,3},... | collective-permute-start | bytes 129032 | tf_op jit(solution)/shard_map/ppermute | solution.py:20
  91.5 5.8 %collective-permute-done.10 = bf16[1,6,3584]{2,1,0:T(8,128)(2,1)S(1)} collective-permute-done((bf16[1,6,3584]{2,1,0:T(8,128)(2,1)S(1)}, bf16[1,6,3584]{2,1,0:T(8,128)(2,1)S(1)}, u32[]{:S(2)}, u32[]{:S(2)}) %collective-permute-start.10) | collective-permute-done | bytes 43040 | tf_op jit(solution)/shard_map/ppermute | solution.py:20
  97.6 2.9 %fusion.3 = f32[96,512]{1,0:T(8,128)S(1)} fusion(bf16[96,3584]{1,0:T(8,128)(2,1)S(1)} %reshape.108, bf16[1,3584,512]{2,1,0:T(8,128)(2,1)} %param.11), kind=kOutput, calls=%fused_computation.11 | convolution fusion | flops 352321536 | bytes 4554752 | tf_op jit(solution)/shard_map/dot_general | solution.py:26
  101.8 3.4 %fusion.8 = f32[96,512]{1,0:T(8,128)S(1)} fusion(bf16[96,3584]{1,0:T(8,128)(2,1)S(1)} %reshape.106, bf16[1,512,3584]{2,1,0:T(8,128)(2,1)} %param.13), kind=kOutput, calls=%fused_computation.16 | convolution fusion | flops 352321536 | bytes 4554752 | tf_op jit(solution)/shard_map/dot_general | solution.py:31
  109.6 6.4 %all-to-all-start.1 = ((bf16[16,6,3584]{2,1,0:T(8,128)(2,1)}), bf16[16,6,3584]{2,1,0:T(8,128)(2,1)S(1)}, u32[]{:S(2)}, u32[]{:S(2)}) async-start(bf16[16,6,3584]{2,1,0:T(8,128)(2,1)} %reshape.109), calls=%async_computation.1 | async-start | bytes 1835008 | tf_op jit(solution)/shard_map/all_to_all | solution.py:104
  118.1 4.2 %convolution_bitcast_fusion = f32[1,512,3584]{2,1,0:T(8,128)} fusion(bf16[96,3584]{1,0:T(8,128)(2,1)S(1)} %reshape.106, f32[96,512]{1,0:T(8,128)S(1)} %fusion.6, f32[96,512]{1,0:T(8,128)S(1)} %fusion.3), kind=kOutput, calls=%fused_computation.5 | convolution fusion | flops 352616448 | bytes 8421376 | tf_op jit(solution)/shard_map/dot_general | solution.py:45
  122.3 16.1 %all-to-all-done.1 = bf16[16,6,3584]{2,1,0:T(8,128)(2,1)S(1)} async-done(((bf16[16,6,3584]{2,1,0:T(8,128)(2,1)}), bf16[16,6,3584]{2,1,0:T(8,128)(2,1)S(1)}, u32[]{:S(2)}, u32[]{:S(2)}) %all-to-all-start.1) | async-done | bytes 688160 | tf_op jit(solution)/shard_map/all_to_all | solution.py:104
  138.8 9.0 %all-reduce = bf16[8,3584]{1,0:T(8,128)(2,1)S(1)} all-reduce(bf16[8,3584]{1,0:T(8,128)(2,1)S(1)} %convolution_convert_fusion), channel_id=2, replica_groups=mesh['sp'=2,'ep'=16] {'sp'}, use_global_device_ids=true, to_apply=%region_5.6.clone | all-reduce | flops 28672 | bytes 114688
  (77 shorter events, 27.1 us)
Async XLA Ops:
  0.6 20.5 %copy-start.3 = (bf16[1,4,3584]{2,1,0:T(4,128)(2,1)S(1)}, bf16[1,4,3584]{2,1,0:T(4,128)(2,1)}, u32[]{:S(2)}) copy-start(bf16[1,4,3584]{2,1,0:T(4,128)(2,1)} %param.8) | copy-start | bytes 86020
  16.6 24.1 %collective-permute-start = (bf16[1,6,3584]{2,1,0:T(8,128)(2,1)S(1)}, bf16[1,6,3584]{2,1,0:T(8,128)(2,1)S(1)}, u32[]{:S(2)}, u32[]{:S(2)}) collective-permute-start(bf16[1,6,3584]{2,1,0:T(8,128)(2,1)S(1)} %get-tuple-element.18), channel_id=1, source_target_pairs={{0,1},{1,0},{2,3},{3,2},{4,5},{5,4},{6,7},{7,6},{8,9},{9,8},{10,11... | collective-permute-start | bytes 129032 | tf_op jit(solution)/shard_map/ppermute | solution.py:20
  30.1 71.4 %all-to-all-start = ((bf16[16,6,3584]{2,1,0:T(8,128)(2,1)}), bf16[16,6,3584]{2,1,0:T(8,128)(2,1)S(1)}, u32[]{:S(2)}, u32[]{:S(2)}) async-start(bf16[16,6,3584]{2,1,0:T(8,128)(2,1)} %reshape.105), calls=%async_computation | async-start | bytes 1835008 | tf_op jit(solution)/shard_map/all_to_all | solution.py:93
  36.3 61.1 %collective-permute-start.14 = (bf16[1,6,3584]{2,1,0:T(8,128)(2,1)S(1)}, bf16[1,6,3584]{2,1,0:T(8,128)(2,1)S(1)}, u32[]{:S(2)}, u32[]{:S(2)}) collective-permute-start(bf16[1,6,3584]{2,1,0:T(8,128)(2,1)S(1)} %get-tuple-element.4), channel_id=1, source_target_pairs={{0,15},{1,14},{2,13},{3,12},{4,11},{5,10},{6,9},{7,8},{8,7},{9,6},... | collective-permute-start | bytes 129032 | tf_op jit(solution)/shard_map/ppermute | solution.py:20
  37.5 59.9 %collective-permute-start.13 = (bf16[1,6,3584]{2,1,0:T(8,128)(2,1)S(1)}, bf16[1,6,3584]{2,1,0:T(8,128)(2,1)S(1)}, u32[]{:S(2)}, u32[]{:S(2)}) collective-permute-start(bf16[1,6,3584]{2,1,0:T(8,128)(2,1)S(1)} %get-tuple-element.5), channel_id=1, source_target_pairs={{0,14},{1,15},{2,12},{3,13},{4,10},{5,11},{6,8},{7,9},{8,6},{9,7},... | collective-permute-start | bytes 129032 | tf_op jit(solution)/shard_map/ppermute | solution.py:20
  38.9 58.4 %collective-permute-start.12 = (bf16[1,6,3584]{2,1,0:T(8,128)(2,1)S(1)}, bf16[1,6,3584]{2,1,0:T(8,128)(2,1)S(1)}, u32[]{:S(2)}, u32[]{:S(2)}) collective-permute-start(bf16[1,6,3584]{2,1,0:T(8,128)(2,1)S(1)} %get-tuple-element.6), channel_id=1, source_target_pairs={{0,13},{1,12},{2,15},{3,14},{4,9},{5,8},{6,11},{7,10},{8,5},{9,4},... | collective-permute-start | bytes 129032 | tf_op jit(solution)/shard_map/ppermute | solution.py:20
  39.2 58.1 %collective-permute-start.11 = (bf16[1,6,3584]{2,1,0:T(8,128)(2,1)S(1)}, bf16[1,6,3584]{2,1,0:T(8,128)(2,1)S(1)}, u32[]{:S(2)}, u32[]{:S(2)}) collective-permute-start(bf16[1,6,3584]{2,1,0:T(8,128)(2,1)S(1)} %get-tuple-element.7), channel_id=1, source_target_pairs={{0,12},{1,13},{2,14},{3,15},{4,8},{5,9},{6,10},{7,11},{8,4},{9,5},... | collective-permute-start | bytes 129032 | tf_op jit(solution)/shard_map/ppermute | solution.py:20
  40.7 5.0 %collective-permute-start.1 = (bf16[1,6,3584]{2,1,0:T(8,128)(2,1)S(1)}, bf16[1,6,3584]{2,1,0:T(8,128)(2,1)S(1)}, u32[]{:S(2)}, u32[]{:S(2)}) collective-permute-start(bf16[1,6,3584]{2,1,0:T(8,128)(2,1)S(1)} %get-tuple-element.17), channel_id=1, source_target_pairs={{0,2},{1,3},{2,0},{3,1},{4,6},{5,7},{6,4},{7,5},{8,10},{9,11},{10,... | collective-permute-start | bytes 129032 | tf_op jit(solution)/shard_map/ppermute | solution.py:20
  45.7 4.4 %collective-permute-start.2 = (bf16[1,6,3584]{2,1,0:T(8,128)(2,1)S(1)}, bf16[1,6,3584]{2,1,0:T(8,128)(2,1)S(1)}, u32[]{:S(2)}, u32[]{:S(2)}) collective-permute-start(bf16[1,6,3584]{2,1,0:T(8,128)(2,1)S(1)} %get-tuple-element.16), channel_id=1, source_target_pairs={{0,3},{1,2},{2,1},{3,0},{4,7},{5,6},{6,5},{7,4},{8,11},{9,10},{10,... | collective-permute-start | bytes 129032 | tf_op jit(solution)/shard_map/ppermute | solution.py:20
  50.1 9.9 %collective-permute-start.3 = (bf16[1,6,3584]{2,1,0:T(8,128)(2,1)S(1)}, bf16[1,6,3584]{2,1,0:T(8,128)(2,1)S(1)}, u32[]{:S(2)}, u32[]{:S(2)}) collective-permute-start(bf16[1,6,3584]{2,1,0:T(8,128)(2,1)S(1)} %get-tuple-element.15), channel_id=1, source_target_pairs={{0,4},{1,5},{2,6},{3,7},{4,0},{5,1},{6,2},{7,3},{8,12},{9,13},{10,... | collective-permute-start | bytes 129032 | tf_op jit(solution)/shard_map/ppermute | solution.py:20
  60.0 3.9 %collective-permute-start.4 = (bf16[1,6,3584]{2,1,0:T(8,128)(2,1)S(1)}, bf16[1,6,3584]{2,1,0:T(8,128)(2,1)S(1)}, u32[]{:S(2)}, u32[]{:S(2)}) collective-permute-start(bf16[1,6,3584]{2,1,0:T(8,128)(2,1)S(1)} %get-tuple-element.14), channel_id=1, source_target_pairs={{0,5},{1,4},{2,7},{3,6},{4,1},{5,0},{6,3},{7,2},{8,13},{9,12},{10,... | collective-permute-start | bytes 129032 | tf_op jit(solution)/shard_map/ppermute | solution.py:20
  64.0 7.0 %collective-permute-start.5 = (bf16[1,6,3584]{2,1,0:T(8,128)(2,1)S(1)}, bf16[1,6,3584]{2,1,0:T(8,128)(2,1)S(1)}, u32[]{:S(2)}, u32[]{:S(2)}) collective-permute-start(bf16[1,6,3584]{2,1,0:T(8,128)(2,1)S(1)} %get-tuple-element.13), channel_id=1, source_target_pairs={{0,6},{1,7},{2,4},{3,5},{4,2},{5,3},{6,0},{7,1},{8,14},{9,15},{10,... | collective-permute-start | bytes 129032 | tf_op jit(solution)/shard_map/ppermute | solution.py:20
  71.0 4.5 %collective-permute-start.6 = (bf16[1,6,3584]{2,1,0:T(8,128)(2,1)S(1)}, bf16[1,6,3584]{2,1,0:T(8,128)(2,1)S(1)}, u32[]{:S(2)}, u32[]{:S(2)}) collective-permute-start(bf16[1,6,3584]{2,1,0:T(8,128)(2,1)S(1)} %get-tuple-element.12), channel_id=1, source_target_pairs={{0,7},{1,6},{2,5},{3,4},{4,3},{5,2},{6,1},{7,0},{8,15},{9,14},{10,... | collective-permute-start | bytes 129032 | tf_op jit(solution)/shard_map/ppermute | solution.py:20
  75.5 5.1 %collective-permute-start.7 = (bf16[1,6,3584]{2,1,0:T(8,128)(2,1)S(1)}, bf16[1,6,3584]{2,1,0:T(8,128)(2,1)S(1)}, u32[]{:S(2)}, u32[]{:S(2)}) collective-permute-start(bf16[1,6,3584]{2,1,0:T(8,128)(2,1)S(1)} %get-tuple-element.11), channel_id=1, source_target_pairs={{0,8},{1,9},{2,10},{3,11},{4,12},{5,13},{6,14},{7,15},{8,0},{9,1},... | collective-permute-start | bytes 129032 | tf_op jit(solution)/shard_map/ppermute | solution.py:20
  80.7 4.8 %collective-permute-start.8 = (bf16[1,6,3584]{2,1,0:T(8,128)(2,1)S(1)}, bf16[1,6,3584]{2,1,0:T(8,128)(2,1)S(1)}, u32[]{:S(2)}, u32[]{:S(2)}) collective-permute-start(bf16[1,6,3584]{2,1,0:T(8,128)(2,1)S(1)} %get-tuple-element.10), channel_id=1, source_target_pairs={{0,9},{1,8},{2,11},{3,10},{4,13},{5,12},{6,15},{7,14},{8,1},{9,0},... | collective-permute-start | bytes 129032 | tf_op jit(solution)/shard_map/ppermute | solution.py:20
  85.5 6.0 %collective-permute-start.9 = (bf16[1,6,3584]{2,1,0:T(8,128)(2,1)S(1)}, bf16[1,6,3584]{2,1,0:T(8,128)(2,1)S(1)}, u32[]{:S(2)}, u32[]{:S(2)}) collective-permute-start(bf16[1,6,3584]{2,1,0:T(8,128)(2,1)S(1)} %get-tuple-element.9), channel_id=1, source_target_pairs={{0,10},{1,11},{2,8},{3,9},{4,14},{5,15},{6,12},{7,13},{8,2},{9,3},... | collective-permute-start | bytes 129032 | tf_op jit(solution)/shard_map/ppermute | solution.py:20
  91.5 5.8 %collective-permute-start.10 = (bf16[1,6,3584]{2,1,0:T(8,128)(2,1)S(1)}, bf16[1,6,3584]{2,1,0:T(8,128)(2,1)S(1)}, u32[]{:S(2)}, u32[]{:S(2)}) collective-permute-start(bf16[1,6,3584]{2,1,0:T(8,128)(2,1)S(1)} %get-tuple-element.8), channel_id=1, source_target_pairs={{0,11},{1,10},{2,9},{3,8},{4,15},{5,14},{6,13},{7,12},{8,3},{9,2},... | collective-permute-start | bytes 129032 | tf_op jit(solution)/shard_map/ppermute | solution.py:20
  97.6 3.1 %copy-start.1 = (bf16[1,3584,512]{2,1,0:T(8,128)(2,1)S(1)}, bf16[1,3584,512]{2,1,0:T(8,128)(2,1)}, u32[]{:S(2)}) copy-start(bf16[1,3584,512]{2,1,0:T(8,128)(2,1)} %param.12) | copy-start | bytes 11010052
  101.7 3.4 %copy-start = (bf16[1,3584,512]{2,1,0:T(8,128)(2,1)S(1)}, bf16[1,3584,512]{2,1,0:T(8,128)(2,1)}, u32[]{:S(2)}) copy-start(bf16[1,3584,512]{2,1,0:T(8,128)(2,1)} %param.11) | copy-start | bytes 11010052
  105.2 2.0 %copy-start.2 = (bf16[1,3584,512]{2,1,0:T(8,128)(2,1)S(1)}, bf16[1,3584,512]{2,1,0:T(8,128)(2,1)}, u32[]{:S(2)}) copy-start(bf16[1,3584,512]{2,1,0:T(8,128)(2,1)} %param.12) | copy-start | bytes 11010052
  107.2 8.9 %copy-start.4 = (u32[32]{0:T(128)S(1)}, u32[32]{0:T(128)}, u32[]{:S(2)}) copy-start(u32[32]{0:T(128)} %constant.77) | copy-start | bytes 388
  109.6 28.8 %all-to-all-start.1 = ((bf16[16,6,3584]{2,1,0:T(8,128)(2,1)}), bf16[16,6,3584]{2,1,0:T(8,128)(2,1)S(1)}, u32[]{:S(2)}, u32[]{:S(2)}) async-start(bf16[16,6,3584]{2,1,0:T(8,128)(2,1)} %reshape.109), calls=%async_computation.1 | async-start | bytes 1835008 | tf_op jit(solution)/shard_map/all_to_all | solution.py:104
